TPU v7x, 256 devices: a whole 4x4x8 slice. The times are simulated.
256 devices in a mesh: wide: 32 (over x, y, core), narrow: 8 (over z).
Axes of the slice: x: 4, y: 4, z: 8, core: 2. Of those that a mesh axis runs over, the one named last changes fastest.
Arguments:
- panels: float32 [256, 512, 512], P('wide', 'narrow'), may hold values from -0.6 to 0.6
- factors: float32 [64, 512, 512], P('wide', 'narrow'), may hold values from -2 to 2
- member: int32 [64, 4], replicated, may hold values from 0 to 255, as said below
- target: int32 [64, 10], replicated, may hold values from 0 to 31
- ancestors: float32 [32, 512, 512], P('wide', 'narrow'), may hold values from -6 to 6
Outputs:
- updated: float32 [32, 512, 512], P('wide', 'narrow')
Inputs may be any that keep to these rules, and one draw needn't show every extreme that they name: `member`: the blocks of supernode s are 4 distinct indices in [(s // 2) * 8, (s // 2 + 1) * 8); every block belongs to exactly one supernode.
All inputs are finite; a program needn't handle non-finite values.
Results may differ from a plain program's by a relative error of at most 0.0003.
Values sent between devices are 32-bit elements; how exact they have to be, the bound alone decides.
No kernel may reach another device: no remote copies, remote signals or barrier semaphores. Data moves between devices by JAX's collectives and lax.ppermute only.
A program may use at most 128 MiB of HBM per device.

v0:
```python
import jax
import jax.numpy as jnp
import numpy as np
from jax import lax
from jax.sharding import PartitionSpec as P


def pair_lists(count):
    left_pick = []
    right_pick = []
    for upper in range(count):
        for lower in range(upper + 1):
            left_pick.append(upper)
            right_pick.append(lower)
    return (np.array(left_pick, dtype=np.int32), np.array(right_pick, dtype=np.int32))


def shards(panels, factors, member, target, ancestors):
    highest = lax.Precision.HIGHEST
    sup_count = factors.shape[0]
    blk_count = panels.shape[0]
    tile_count = ancestors.shape[0] * lax.axis_size("wide")
    left_pick, right_pick = pair_lists(member.shape[1])
    owner_index = lax.axis_index("wide")
    own_members = (
        lax.dynamic_slice_in_dim(member, owner_index * sup_count, sup_count, 0)
        - owner_index * blk_count
    )
    own_targets = lax.dynamic_slice_in_dim(target, owner_index * sup_count, sup_count, 0)
    full_factors = lax.all_gather(factors, "narrow", axis=1, tiled=True)
    blocks = panels[own_members]
    scaled = jnp.einsum("skrw,swv->skrv", blocks, full_factors, precision=highest)
    left_rows = scaled[:, left_pick]
    right_rows = lax.all_gather(scaled, "narrow", axis=2, tiled=True)[:, right_pick]
    updates = jnp.einsum("sprv,spmv->sprm", left_rows, right_rows, precision=highest)
    tile_ids = jnp.arange(tile_count, dtype=jnp.int32)
    onehot = (own_targets[:, :, None] == tile_ids[None, None, :]).astype(jnp.float32)
    portion = jnp.einsum("spa,sprw->arw", onehot, updates, precision=highest)
    totals = lax.psum_scatter(portion, "wide", scatter_dimension=0, tiled=True)
    return ancestors - totals


def solution(mesh):
    return jax.shard_map(
        shards,
        mesh=mesh,
        in_specs=(
            P("wide", "narrow", None),
            P("wide", "narrow", None),
            P(),
            P(),
            P("wide", "narrow", None),
        ),
        out_specs=P("wide", "narrow", None),
        check_vma=False,
    )
```

profile of v0, /device:TPU:2, one launch (start us, length us, event | category | flops | bytes accessed | tf_op | source)
XLA Modules:
  0.0 293.5 jit_solution(6393277430765025806)
XLA Ops:
  6.5 0.0 copy-start
  6.5 0.0 all-gather.3.cloned.1.call-start
  6.5 0.7 all-gather.3.cloned.1.call-update
  7.3 0.0 all-gather.5.cloned.1.call-start
  7.3 0.8 compare_select_fusion
  8.1 0.1 copy.15
  8.2 0.1 reshape.3
  8.3 0.0 copy-done
  8.3 0.6 gather_fusion
  8.9 44.1 %all-gather.3.cloned.1.call-done = f32[2,512,512]{2,1,0:T(8,128)} async-done(((f32[2,64,512]{2,1,0:T(8,128)}), f32[2,512,512]{2,1,0:T(8,128)}) %all-gather.3.cloned.1.call-update) | async-done | bytes 2097168 | tf_op jit(solution)/shard_map/all_gather | solution.py:30
  53.0 0.0 copy-start.3
  53.0 0.0 copy-start.5
  53.0 0.0 copy-start.4
  53.0 4.5 %fusion.8 = f32[2,4,64,512]{3,2,1,0:T(8,128)} fusion(f32[2,4,64,512]{3,2,1,0:T(8,128)S(1)} %bitcast.21, f32[2,512,512]{2,1,0:T(8,128)} %all-gather.3.cloned.1.call-done), kind=kOutput, calls=%fused_computation.9 | convolution fusion | flops 1610612736 | bytes 4194304 | tf_op jit(solution)/shard_map/skrw,swv->skrv/dot_general | solution.py:32
  57.5 0.0 copy-start.1
  57.5 0.0 all-gather.5.cloned.1.call-update
  57.6 0.0 reduce-scatter.2.cloned.1.call-start
  57.6 0.0 copy-done.3
  57.6 0.1 constant_dynamic-slice_fusion
  57.7 0.1 copy.14
  57.8 0.0 copy-done.5
  57.8 0.0 copy-done.4
  57.8 0.9 copy-done.1
  58.8 2.2 gather_fusion.1
  60.9 89.4 %all-gather.5.cloned.1.call-done = f32[2,4,512,512]{3,2,1,0:T(8,128)} async-done(((f32[2,4,64,512]{3,2,1,0:T(8,128)}), f32[2,4,512,512]{3,2,1,0:T(8,128)}) %all-gather.5.cloned.1.call-update) | async-done | bytes 8388624 | tf_op jit(solution)/shard_map/all_gather | solution.py:34
  150.3 12.6 %gather_fusion.2 = f32[10,2,512,512]{3,2,1,0:T(8,128)} fusion(f32[2,4,512,512]{3,2,1,0:T(8,128)} %all-gather.5.cloned.1.call-done, s32[1024]{0:T(1024)S(1)} %pad_clamp_fusion), kind=kCustom, calls=%fused_computation.2 | custom fusion | bytes 41943080 | tf_op jit(solution)/shard_map/gather | solution.py:34
  162.9 25.8 %fusion = f32[2,10,64,512]{3,2,1,0:T(8,128)S(1)} fusion(f32[10,2,512,512]{3,2,1,0:T(8,128)} %gather_fusion.2, f32[10,2,64,512]{3,2,1,0:T(8,128)} %gather_fusion.1), kind=kOutput, calls=%fused_computation.3 | convolution fusion | flops 4026531840 | bytes 26214400 | tf_op jit(solution)/shard_map/sprv,spmv->sprm/dot_general | solution.py:35
  188.7 3.9 %fusion.5 = f32[32,64,512]{2,0,1:T(8,128)S(1)} fusion(f32[2,10,64,512]{3,2,1,0:T(8,128)S(1)} %fusion, s32[2,10]{1,0:T(2,128)S(1)} %copy.14), kind=kOutput, calls=%fused_computation.8 | convolution fusion | flops 251658880 | bytes 6815824 | tf_op jit(solution)/shard_map/spa,sprw->arw/dot_general | solution.py:38
  192.6 4.4 %copy.16 = f32[32,64,512]{2,1,0:T(8,128)} copy(f32[32,64,512]{2,0,1:T(8,128)S(1)} %fusion.5) | data formatting | bytes 8388608 | tf_op jit(solution)/shard_map/spa,sprw->arw/dot_general | solution.py:38
  197.0 0.0 copy-start.2
  197.0 0.0 reduce-scatter.2.cloned.1.call-update
  197.0 88.4 %reduce-scatter.2.cloned.1.call-done = f32[1,64,512]{2,1,0:T(8,128)} async-done(((f32[32,64,512]{2,1,0:T(8,128)}), f32[1,64,512]{2,1,0:T(8,128)}) %reduce-scatter.2.cloned.1.call-update) | async-done | bytes 131088 | tf_op jit(solution)/shard_map/reduce_scatter | solution.py:39
  285.4 0.0 copy-done.2
  285.4 1.6 sub.11
  (3 shorter events, 0.0 us)
Async XLA Ops:
  6.5 1.7 copy-start
  6.5 46.4 %all-gather.3.cloned.1.call-start = ((), (), s32[]{:S(2)}) async-start(), calls=%async_computation.1 | async-start | bytes 2359296 | tf_op jit(solution)/shard_map/all_gather | solution.py:30
  7.3 143.1 %all-gather.5.cloned.1.call-start = ((), (), s32[]{:S(2)}) async-start(), calls=%async_computation.2 | async-start | bytes 9437184 | tf_op jit(solution)/shard_map/all_gather | solution.py:34
  53.0 4.6 %copy-start.3 = (s32[64,10]{0,1:T(8,128)S(1)}, s32[64,10]{0,1:T(8,128)}, u32[]{:S(2)}) copy-start(s32[64,10]{0,1:T(8,128)} %param.12) | copy-start | bytes 7684
  53.0 4.8 %copy-start.5 = (s32[10]{0:T(128)S(1)}, s32[10]{0:T(128)}, u32[]{:S(2)}) copy-start(s32[10]{0:T(128)} %constant.33) | copy-start | bytes 124
  53.0 4.8 %copy-start.4 = (s32[10]{0:T(128)S(1)}, s32[10]{0:T(128)}, u32[]{:S(2)}) copy-start(s32[10]{0:T(128)} %constant.32) | copy-start | bytes 124
  57.5 1.2 copy-start.1
  57.6 227.9 %reduce-scatter.2.cloned.1.call-start = ((), (), s32[]{:S(2)}) async-start(), calls=%async_computation.3 | async-start | bytes 4325376 | tf_op jit(solution)/shard_map/reduce_scatter | solution.py:39
  197.0 88.4 %copy-start.2 = (f32[1,64,512]{2,1,0:T(8,128)S(1)}, f32[1,64,512]{2,1,0:T(8,128)}, u32[]{:S(2)}) copy-start(f32[1,64,512]{2,1,0:T(8,128)} %param.13) | copy-start | bytes 393220
Sparse Core Ops, SparseCore 0:
  9.1 43.8 all-gather.2
  57.7 92.6 all-gather.4
  197.1 88.2 reduce-scatter.1
where the time goes:
time: 294 us
  waiting for transfers between devices  223 us (76%)
  matrix products  34.2 us (12%)
  local copies, waits for them, and re-layouts  21.1 us (7%)
  between operations  13.2 us (4%)
    all_gather x1, waiting for transfers between devices, shards(): lax.all_gather(scaled, 'narrow', axis=2, tiled=True)[:, right_pick]  89.4 us
    reduce_scatter x1, waiting for transfers between devices, shards(): totals = lax.psum_scatter(portion, 'wide', scatter_dimension=0, tiled=True)  88.4 us
    all_gather x1, waiting for transfers between devices, shards(): full_factors = lax.all_gather(factors, 'narrow', axis=1, tiled=True)  44.1 us
    dot_general x1, matrix products, shards(): jnp.einsum('sprv,spmv->sprm', left_rows, right_rows, precision=highest)  25.8 us
    gather x1, local copies, waits for them, and re-layouts, shards(): lax.all_gather(scaled, 'narrow', axis=2, tiled=True)[:, right_pick]  12.6 us
  transfers between devices with their start and end apart: 3, of which 3 were waited for; matrix products, arithmetic and copies ran while one was open for 1% of the time, Pallas kernels for 0%

commit v1 on v0

--- a/solution.py
+++ b/solution.py
@@ -3,6 +3,11 @@
 import numpy as np
 from jax import lax
 from jax.sharding import PartitionSpec as P
+
+
+def all_by_exchange(value, axis, d):
+    sent = jnp.stack([value] * lax.axis_size(axis))
+    return jnp.concatenate(lax.all_to_all(sent, axis, 0, 0), axis=d)
 
 
 def pair_lists(count):
@@ -31,7 +36,7 @@
     blocks = panels[own_members]
     scaled = jnp.einsum("skrw,swv->skrv", blocks, full_factors, precision=highest)
     left_rows = scaled[:, left_pick]
-    right_rows = lax.all_gather(scaled, "narrow", axis=2, tiled=True)[:, right_pick]
+    right_rows = all_by_exchange(scaled, "narrow", 2)[:, right_pick]
     updates = jnp.einsum("sprv,spmv->sprm", left_rows, right_rows, precision=highest)
     tile_ids = jnp.arange(tile_count, dtype=jnp.int32)
     onehot = (own_targets[:, :, None] == tile_ids[None, None, :]).astype(jnp.float32)

time: 294 us -> 398 us (1.35)
  waiting for transfers between devices: 223 us -> 310 us
  local copies, waits for them, and re-layouts: 21.1 us -> 33 us
  starting transfers between devices: 0.08 us -> 5.3 us
    all_to_all x0 -> x1, waiting for transfers between devices: none -> 180 us  [all_by_exchange(): return jnp.concatenate(lax.all_to_all(sent, axis, 0, 0), axis=d)]
    all_gather x1 -> x0, waiting for transfers between devices: 89.4 us -> none  [shards(): lax.all_gather(scaled, 'narrow', axis=2, tiled=True)[:, right_pick]]
    all_to_all x0 -> x1, local copies, waits for them, and re-layouts: none -> 8.46 us  [all_by_exchange(): return jnp.concatenate(lax.all_to_all(sent, axis, 0, 0), axis=d)]
    all_to_all x0 -> x1, starting transfers between devices: none -> 5.08 us  [all_by_exchange(): return jnp.concatenate(lax.all_to_all(sent, axis, 0, 0), axis=d)]
    another operation x0 -> x1, local copies, waits for them, and re-layouts: none -> 4.33 us  [all_by_exchange(): sent = jnp.stack([value] * lax.axis_size(axis))]
where the time goes in v1:
time: 398 us
  waiting for transfers between devices  310 us (78%)
  matrix products  33.2 us (8%)
  local copies, waits for them, and re-layouts  33 us (8%)
  between operations  13.5 us (3%)
  starting transfers between devices  5.3 us (1%)
    all_to_all x1, waiting for transfers between devices, all_by_exchange(): return jnp.concatenate(lax.all_to_all(sent, axis, 0, 0), axis=d)  180 us
    reduce_scatter x1, waiting for transfers between devices, shards(): totals = lax.psum_scatter(portion, 'wide', scatter_dimension=0, tiled=True)  85.8 us
    all_gather x1, waiting for transfers between devices, shards(): full_factors = lax.all_gather(factors, 'narrow', axis=1, tiled=True)  44.1 us
    dot_general x1, matrix products, shards(): jnp.einsum('sprv,spmv->sprm', left_rows, right_rows, precision=highest)  25.8 us
    gather x1, local copies, waits for them, and re-layouts, shards(): right_rows = all_by_exchange(scaled, 'narrow', 2)[:, right_pick]  12.6 us
    all_to_all x1, local copies, waits for them, and re-layouts, all_by_exchange(): return jnp.concatenate(lax.all_to_all(sent, axis, 0, 0), axis=d)  8.46 us
  transfers between devices with their start and end apart: 3, of which 3 were waited for; matrix products, arithmetic and copies ran while one was open for 1% of the time, Pallas kernels for 0%

profile of v1, /device:TPU:2, one launch (start us, length us, event | category | flops | bytes accessed | tf_op | source)
XLA Modules:
  0.0 397.8 jit_solution(17353954467687986533)
XLA Ops:
  6.5 0.0 copy-start
  6.5 0.0 all-gather.2.cloned.1.call-start
  6.5 0.7 all-gather.2.cloned.1.call-update
  7.3 0.8 compare_select_fusion
  8.0 0.1 copy.19
  8.1 0.1 reshape.13
  8.2 0.0 copy-done
  8.2 0.6 gather_fusion
  8.8 44.1 %all-gather.2.cloned.1.call-done = f32[2,512,512]{2,1,0:T(8,128)} async-done(((f32[2,64,512]{2,1,0:T(8,128)}), f32[2,512,512]{2,1,0:T(8,128)}) %all-gather.2.cloned.1.call-update) | async-done | bytes 2097168 | tf_op jit(solution)/shard_map/all_gather | solution.py:35
  53.0 3.5 fusion.8
  56.5 4.3 %stack.2 = f32[8,2,4,64,512]{4,3,2,1,0:T(8,128)} broadcast(f32[2,4,64,512]{3,2,1,0:T(8,128)S(1)} %fusion.8), dimensions={1,2,3,4} | broadcast | bytes 9437184 | tf_op jit(solution)/shard_map/stack | solution.py:9
  60.8 0.0 copy-start.2
  60.8 0.0 copy-start.4
  60.8 0.0 copy-start.3
  60.8 5.1 %all-to-all-start = ((f32[8,2,4,64,512]{4,3,2,1,0:T(8,128)}), f32[8,2,4,64,512]{4,3,2,1,0:T(8,128)}, u32[]{:S(2)}, u32[]{:S(2)}) async-start(f32[8,2,4,64,512]{4,3,2,1,0:T(8,128)} %stack.2), calls=%async_computation | async-start | bytes 16777216 | tf_op jit(solution)/shard_map/all_to_all | solution.py:10
  65.9 0.2 reduce-scatter.2.cloned.1.call-start
  66.2 0.0 copy-done.2
  66.2 0.1 constant_dynamic-slice_fusion
  66.2 0.1 copy.18
  66.3 0.0 copy-done.4
  66.3 0.0 copy-done.3
  66.4 2.2 gather_fusion.1
  68.6 179.8 %all-to-all-done = f32[8,2,4,64,512]{4,3,2,1,0:T(8,128)} async-done(((f32[8,2,4,64,512]{4,3,2,1,0:T(8,128)}), f32[8,2,4,64,512]{4,3,2,1,0:T(8,128)}, u32[]{:S(2)}, u32[]{:S(2)}) %all-to-all-start) | async-done | bytes 8388640 | tf_op jit(solution)/shard_map/all_to_all | solution.py:10
  248.3 8.5 %copy.20 = f32[8,2,4,64,512]{4,3,0,2,1:T(8,128)} copy(f32[8,2,4,64,512]{4,3,2,1,0:T(8,128)} %all-to-all-done) | data formatting | bytes 16777216 | tf_op jit(solution)/shard_map/all_to_all | solution.py:10
  256.8 12.6 %gather_fusion.2 = f32[10,2,512,512]{3,2,1,0:T(8,128)} fusion(f32[2,4,512,512]{3,2,1,0:T(8,128)} %bitcast.24, s32[1024]{0:T(1024)S(1)} %pad_clamp_fusion), kind=kCustom, calls=%fused_computation.2 | custom fusion | bytes 41943080 | tf_op jit(solution)/shard_map/gather | solution.py:39
  269.4 25.8 %fusion = f32[2,10,64,512]{3,2,1,0:T(8,128)S(1)} fusion(f32[10,2,512,512]{3,2,1,0:T(8,128)} %gather_fusion.2, f32[10,2,64,512]{3,2,1,0:T(8,128)} %gather_fusion.1), kind=kOutput, calls=%fused_computation.3 | convolution fusion | flops 4026531840 | bytes 26214400 | tf_op jit(solution)/shard_map/sprv,spmv->sprm/dot_general | solution.py:40
  295.2 3.9 fusion.5
  299.1 4.4 %copy.24 = f32[32,64,512]{2,1,0:T(8,128)} copy(f32[32,64,512]{2,0,1:T(8,128)S(1)} %fusion.5) | data formatting | bytes 8388608 | tf_op jit(solution)/shard_map/spa,sprw->arw/dot_general | solution.py:43
  303.5 0.0 copy-start.1
  303.5 0.0 reduce-scatter.2.cloned.1.call-update
  303.5 85.8 %reduce-scatter.2.cloned.1.call-done = f32[1,64,512]{2,1,0:T(8,128)} async-done(((f32[32,64,512]{2,1,0:T(8,128)}), f32[1,64,512]{2,1,0:T(8,128)}) %reduce-scatter.2.cloned.1.call-update) | async-done | bytes 131088 | tf_op jit(solution)/shard_map/reduce_scatter | solution.py:44
  389.4 0.0 copy-done.1
  389.4 1.6 sub.11
  (3 shorter events, 0.0 us)
Async XLA Ops:
  6.5 1.7 copy-start
  6.5 46.4 %all-gather.2.cloned.1.call-start = ((), (), s32[]{:S(2)}) async-start(), calls=%async_computation.2 | async-start | bytes 2359296 | tf_op jit(solution)/shard_map/all_gather | solution.py:35
  60.8 5.3 %copy-start.2 = (s32[64,10]{0,1:T(8,128)S(1)}, s32[64,10]{0,1:T(8,128)}, u32[]{:S(2)}) copy-start(s32[64,10]{0,1:T(8,128)} %param.12) | copy-start | bytes 7684
  60.8 5.5 %copy-start.4 = (s32[10]{0:T(128)S(1)}, s32[10]{0:T(128)}, u32[]{:S(2)}) copy-start(s32[10]{0:T(128)} %constant.33) | copy-start | bytes 124
  60.8 5.5 %copy-start.3 = (s32[10]{0:T(128)S(1)}, s32[10]{0:T(128)}, u32[]{:S(2)}) copy-start(s32[10]{0:T(128)} %constant.32) | copy-start | bytes 124
  60.8 187.5 %all-to-all-start = ((f32[8,2,4,64,512]{4,3,2,1,0:T(8,128)}), f32[8,2,4,64,512]{4,3,2,1,0:T(8,128)}, u32[]{:S(2)}, u32[]{:S(2)}) async-start(f32[8,2,4,64,512]{4,3,2,1,0:T(8,128)} %stack.2), calls=%async_computation | async-start | bytes 16777216 | tf_op jit(solution)/shard_map/all_to_all | solution.py:10
  65.9 323.4 %reduce-scatter.2.cloned.1.call-start = ((), (), s32[]{:S(2)}) async-start(), calls=%async_computation.3 | async-start | bytes 4325376 | tf_op jit(solution)/shard_map/reduce_scatter | solution.py:44
  303.5 85.9 %copy-start.1 = (f32[1,64,512]{2,1,0:T(8,128)S(1)}, f32[1,64,512]{2,1,0:T(8,128)}, u32[]{:S(2)}) copy-start(f32[1,64,512]{2,1,0:T(8,128)} %param.13) | copy-start | bytes 393220
Sparse Core Ops, SparseCore 0:
  9.1 43.8 all-gather.1
  303.6 85.6 reduce-scatter.1
